TPU v7x, 32 devices: a whole 2x2x4 slice. The times are simulated.
32 devices in a mesh: row: 4 (over z), col: 8 (over y, x, core).
Axes of the slice: x: 2, y: 2, z: 4, core: 2. Of those that a mesh axis runs over, the one named last changes fastest.
Arguments:
- hessian: float32 [16384, 4, 8, 512], P('row', None, 'col'), may hold values from -1 to 16, as said below
- weights: bfloat16 [512, 16384], P('col', 'row'), may hold values from -6 to 6
- codes: int32 [512, 8192], P('col', 'row'), may hold values from 0 to 255
- tile_map: int32 [32, 64], P('col', 'row'), may hold values from 0 to 511
- codebooks: float32 [512, 2, 256], replicated, may hold values from -6 to 6
Outputs:
- adjusted_codebooks: float32 [512, 2, 256], replicated
Inputs may be any that keep to these rules, and one draw needn't show every extreme that they name: `hessian`: H is symmetric with a dominant positive diagonal.
All inputs are finite; a program needn't handle non-finite values.
Results may differ from a plain program's by a relative error of at most 0.0003.
Values sent between devices are 32-bit elements; how exact they have to be, the bound alone decides.
A program may use at most 192 MiB of HBM per device.

v0:
```python
import jax
import jax.numpy as jnp
from jax import lax
from jax.sharding import PartitionSpec as P

CODES = 256
NB = 512
TILE_ROWS = 16
TILE_COLS = 256
STEPS = 2
learn_rate = 0.01


def per_device(hessian, weights, codes, tile_map, codebooks):
    rows_local, cols_local = weights.shape
    rows_tiles = rows_local // TILE_ROWS
    cols_tiles = cols_local // TILE_COLS
    tile_count = rows_tiles * cols_tiles
    half_width = TILE_COLS // 2
    pair_count = TILE_ROWS * half_width
    hessian_tile = hessian.reshape(
        hessian.shape[0], hessian.shape[1] * hessian.shape[2] * hessian.shape[3]
    )
    code_tiles = (
        codes.reshape(rows_tiles, TILE_ROWS, cols_tiles, half_width)
        .transpose(0, 2, 1, 3)
        .reshape(tile_count, pair_count)
    )
    code_onehot = (
        code_tiles[:, :, None] == lax.broadcasted_iota(jnp.int32, (1, 1, CODES), 2)
    ).astype(jnp.float32)
    book_onehot = (
        tile_map.reshape(-1)[:, None] == lax.broadcasted_iota(jnp.int32, (1, NB), 1)
    ).astype(jnp.float32)
    for iteration in range(STEPS):
        tile_books = jnp.einsum(
            "tb,bck->tck", book_onehot, codebooks, precision=lax.Precision.HIGHEST
        )
        rebuilt_tiles = jnp.einsum(
            "tpk,tck->tpc", code_onehot, tile_books, precision=lax.Precision.HIGHEST
        )
        rebuilt = (
            rebuilt_tiles.reshape(rows_tiles, cols_tiles, TILE_ROWS, half_width, 2)
            .transpose(0, 2, 1, 3, 4)
            .reshape(rows_local, cols_local)
        )
        error = rebuilt - weights.astype(jnp.float32)
        error_piece = lax.all_to_all(error, "col", split_axis=1, concat_axis=0, tiled=True)
        error_spread = lax.all_gather(error_piece, "row", axis=1, tiled=True)
        weight_grad = 2.0 * lax.psum_scatter(
            lax.dot_general(
                error_spread,
                hessian_tile,
                (((1,), (1,)), ((), ())),
                precision=lax.Precision.HIGHEST,
                preferred_element_type=jnp.float32,
            ),
            "col",
            scatter_dimension=0,
            tiled=True,
        )
        grad_tiles = (
            weight_grad.reshape(rows_tiles, TILE_ROWS, cols_tiles, half_width, 2)
            .transpose(0, 2, 1, 3, 4)
            .reshape(tile_count, pair_count, 2)
        )
        tile_grads = jnp.einsum(
            "tpk,tpc->tck", code_onehot, grad_tiles, precision=lax.Precision.HIGHEST
        )
        local_grad = jnp.einsum(
            "tb,tck->bck", book_onehot, tile_grads, precision=lax.Precision.HIGHEST
        )
        total_even, total_odd = lax.psum((local_grad[:, 0, :], local_grad[:, 1, :]), ("row", "col"))
        book_grad = jnp.stack([total_even, total_odd], axis=1)
        codebooks = codebooks - learn_rate * book_grad
    return codebooks


def solution(mesh):
    placed = (P("row", None, "col", None), P("col", "row"), P("col", "row"), P("col", "row"), P())
    return jax.shard_map(per_device, mesh=mesh, in_specs=placed, out_specs=P(), check_vma=False)
```

profile of v0, /device:TPU:0, one launch (start us, length us, event | category | flops | bytes accessed | tf_op | source)
XLA Modules:
  0.0 1101.7 jit_solution(13116930296548509444)
XLA Ops:
  10.8 68.2 %fusion.3 = f32[64,2048,2]{1,2,0:T(2,128)S(1)} fusion(s32[64,2048]{1,0:T(8,128)S(1)} %bitcast.70, f32[64,2,256]{2,0,1:T(8,128)S(1)} %fusion.10), kind=kOutput, calls=%fused_computation.4 | convolution fusion | flops 838860800 | bytes 1703936 | tf_op jit(solution)/shard_map/tpk,tck->tpc/dot_general | solution.py:39
  80.3 5.8 copy.11
  86.1 6.5 reshape.40
  96.3 20.4 %all_to_all.38 = f32[64,8,512]{2,0,1:T(8,128)} all-to-all(f32[64,8,512]{2,0,1:T(8,128)S(1)} %copy.13), channel_id=1, replica_groups=mesh['row'=4,'col'=8] {'col'}, dimensions={1} | all-to-all | bytes 2097152 | tf_op jit(solution)/shard_map/all_to_all | solution.py:48
  117.0 101.8 %reduce = f32[4096,4,512]{2,1,0:T(4,128)} reduce(f32[4096,4,1,512]{3,2,1,0:T(1,128)} %param.5, f32[]{:T(128)} %constant.6), dimensions={2}, to_apply=%param.5.reduce_sub_computation | reduce | bytes 67108864 | tf_op args[0]
  218.8 29.9 %copy.34 = f32[512,8,4,512]{3,1,2,0:T(8,128)} copy(f32[512,8,4,512]{3,2,1,0:T(4,128)} %bitcast.56) | data formatting | bytes 67108864
  248.7 59.3 %fusion.33 = f32[512,4096]{1,0:T(8,128)} fusion(f32[512,2048]{1,0:T(8,128)} %all-gather.3.cloned.1.call-done, f32[4096,2048]{1,0:T(8,128)} %bitcast.61), kind=kOutput, calls=%fused_computation.37 | convolution fusion | flops 51539607552 | bytes 46137344 | tf_op jit(solution)/shard_map/dot_general | solution.py:51
  308.1 71.0 %reduce-scatter.3.cloned.1.call-done = f32[64,4096]{1,0:T(8,128)} async-done(((f32[512,4096]{1,0:T(8,128)}), f32[64,4096]{1,0:T(8,128)}) %reduce-scatter.3.cloned.1.call-update) | async-done | bytes 1048592 | tf_op jit(solution)/shard_map/reduce_scatter | solution.py:50
  383.2 5.5 reshape.42
  388.7 6.7 copy.28
  395.9 46.3 %fusion.2 = f32[64,2,256]{2,1,0:T(2,128)S(1)} fusion(f32[64,2048,2]{1,2,0:T(2,128)S(1)} %reshape.53, s32[64,2048]{1,0:T(8,128)} %bitcast.71), kind=kOutput, calls=%fused_computation.3 | convolution fusion | flops 838860800 | bytes 1703936 | tf_op jit(solution)/shard_map/tpk,tpc->tck/dot_general | solution.py:67
  444.2 131.0 %all-reduce.7.cloned.1.call-done = (f32[512,1,256]{2,0,1:T(8,128)}, f32[512,1,256]{2,0,1:T(8,128)}) async-done(((f32[512,1,256]{2,0,1:T(8,128)}, f32[512,1,256]{2,0,1:T(8,128)}), (f32[512,1,256]{2,0,1:T(8,128)}, f32[512,1,256]{2,0,1:T(8,128)})) %all-reduce.7.cloned.1.call-update) | async-done | bytes 1048592 | tf_op jit(solution)/shard_map/psum | solution.py:73
  577.0 69.8 %fusion.1 = f32[64,2048,2]{1,2,0:T(2,128)} fusion(s32[64,2048]{1,0:T(8,128)} %bitcast.72, f32[64,2,256]{2,0,1:T(8,128)S(1)} %fusion.12), kind=kOutput, calls=%fused_computation.2 | convolution fusion | flops 838860800 | bytes 1703936 | tf_op jit(solution)/shard_map/tpk,tck->tpc/dot_general | solution.py:39
  648.8 5.8 copy.17
  654.6 7.6 reshape.45
  662.2 3.1 convert_subtract_fusion
  667.6 18.8 %all_to_all.39 = f32[64,8,512]{2,0,1:T(8,128)} all-to-all(f32[64,8,512]{2,0,1:T(8,128)S(1)} %copy.18), channel_id=1, replica_groups=mesh['row'=4,'col'=8] {'col'}, dimensions={1} | all-to-all | bytes 2097152 | tf_op jit(solution)/shard_map/all_to_all | solution.py:48
  686.5 78.5 %all-gather.5.cloned.1.call-done = f32[512,2048]{1,0:T(8,128)} async-done(((f32[512,512]{1,0:T(8,128)}), f32[512,2048]{1,0:T(8,128)}) %all-gather.5.cloned.1.call-update) | async-done | bytes 4194320 | tf_op jit(solution)/shard_map/all_gather | solution.py:49
  764.9 59.3 %fusion.34 = f32[512,4096]{1,0:T(8,128)} fusion(f32[512,2048]{1,0:T(8,128)} %all-gather.5.cloned.1.call-done, f32[4096,2048]{1,0:T(8,128)} %bitcast.62), kind=kOutput, calls=%fused_computation.38 | convolution fusion | flops 51539607552 | bytes 46137344 | tf_op jit(solution)/shard_map/dot_general | solution.py:51
  824.6 69.8 %reduce-scatter.5.cloned.1.call-done = f32[64,4096]{1,0:T(8,128)} async-done(((f32[512,4096]{1,0:T(8,128)}), f32[64,4096]{1,0:T(8,128)}) %reduce-scatter.5.cloned.1.call-update) | async-done | bytes 1048592 | tf_op jit(solution)/shard_map/reduce_scatter | solution.py:50
  897.7 7.3 reshape.46
  905.0 6.7 copy.29
  912.2 46.3 %fusion = f32[64,2,256]{2,1,0:T(2,128)S(1)} fusion(f32[64,2048,2]{1,2,0:T(2,128)S(1)} %reshape.54, s32[64,2048]{1,0:T(8,128)} %bitcast.73), kind=kOutput, calls=%fused_computation.1 | convolution fusion | flops 838860800 | bytes 1703936 | tf_op jit(solution)/shard_map/tpk,tpc->tck/dot_general | solution.py:67
  960.3 131.3 %all-reduce.5.cloned.1.call-done = (f32[512,1,256]{2,0,1:T(8,128)}, f32[512,1,256]{2,0,1:T(8,128)}) async-done(((f32[512,1,256]{2,0,1:T(8,128)}, f32[512,1,256]{2,0,1:T(8,128)}), (f32[512,1,256]{2,0,1:T(8,128)}, f32[512,1,256]{2,0,1:T(8,128)})) %all-reduce.5.cloned.1.call-update) | async-done | bytes 1048592 | tf_op jit(solution)/shard_map/psum | solution.py:73
  (47 shorter events, 31.4 us)
Async XLA Ops:
  6.5 242.2 %all-gather.3.cloned.1.call-start = ((), (), s32[]{:S(2)}) async-start(), calls=%async_computation.4 | async-start | bytes 5242880 | tf_op jit(solution)/shard_map/all_gather | solution.py:49
  8.8 2.0 copy-start.4
  10.8 69.1 %copy-start.3 = (bf16[64,4096]{1,0:T(8,128)(2,1)S(1)}, bf16[64,4096]{1,0:T(8,128)(2,1)}, u32[]{:S(2)}) copy-start(bf16[64,4096]{1,0:T(8,128)(2,1)} %param.6) | copy-start | bytes 1572868
  116.8 262.3 %reduce-scatter.3.cloned.1.call-start = ((), (), s32[]{:S(2)}) async-start(), calls=%async_computation.5 | async-start | bytes 9437184 | tf_op jit(solution)/shard_map/reduce_scatter | solution.py:50
  308.1 267.1 %all-reduce.7.cloned.1.call-start = ((), (), s32[]{:S(2)}) async-start(), calls=%async_computation.9 | async-start | bytes 2097152 | tf_op jit(solution)/shard_map/psum | solution.py:73
  395.9 179.3 %copy-start = (f32[512,2,256]{2,1,0:T(2,128)S(1)}, f32[512,2,256]{2,1,0:T(2,128)}, u32[]{:S(2)}) copy-start(f32[512,2,256]{2,1,0:T(2,128)} %param.9) | copy-start | bytes 3145732
  444.0 321.0 %all-gather.5.cloned.1.call-start = ((), (), s32[]{:S(2)}) async-start(), calls=%async_computation.6 | async-start | bytes 5242880 | tf_op jit(solution)/shard_map/all_gather | solution.py:49
  686.4 208.0 %reduce-scatter.5.cloned.1.call-start = ((), (), s32[]{:S(2)}) async-start(), calls=%async_computation.7 | async-start | bytes 9437184 | tf_op jit(solution)/shard_map/reduce_scatter | solution.py:50
  824.3 267.3 %all-reduce.5.cloned.1.call-start = ((), (), s32[]{:S(2)}) async-start(), calls=%async_computation.8 | async-start | bytes 2097152 | tf_op jit(solution)/shard_map/psum | solution.py:73
  912.2 179.4 %copy-start.1 = (f32[512,1,256]{2,0,1:T(8,128)S(1)}, f32[512,1,256]{2,0,1:T(8,128)}, u32[]{:S(2)}) copy-start(f32[512,1,256]{2,0,1:T(8,128)} %get-tuple-element.7) | copy-start | bytes 1572868
  912.2 179.4 %copy-start.2 = (f32[512,1,256]{2,0,1:T(8,128)S(1)}, f32[512,1,256]{2,0,1:T(8,128)}, u32[]{:S(2)}) copy-start(f32[512,1,256]{2,0,1:T(8,128)} %get-tuple-element.8) | copy-start | bytes 1572868
Sparse Core Ops, SparseCore 0:
  116.9 80.0 all-gather.2
  308.2 70.8 reduce-scatter.2
  444.1 131.0 all-reduce.6
  686.5 78.3 all-gather.4
  824.4 69.9 reduce-scatter.4
  960.4 131.1 all-reduce.4
where the time goes:
time: 1100 us
  waiting for transfers between devices  482 us (44%)
  matrix products  354 us (32%)
  other arithmetic  111 us (10%)
  local copies, waits for them, and re-layouts  100 us (9%)
  blocking collectives  39.3 us (4%)
  between operations  13.7 us (1%)
    psum x2, waiting for transfers between devices, per_device(): lax.psum((local_grad[:, 0, :], local_grad[:, 1, :]), ('row', 'col'))  262 us
    reduce_scatter x2, waiting for transfers between devices, per_device(): lax.psum_scatter(lax.dot_general(error_spread, hessian_tile, (((1,), (1,)...  141 us
    dot_general x2, matrix products, per_device(): jnp.einsum('tpk,tck->tpc', code_onehot, tile_books, precision=lax.Precisi...  138 us
    dot_general x2, matrix products, per_device(): lax.dot_general(error_spread, hessian_tile, (((1,), (1,)), ((), ())), pre...  119 us
    unnamed x1, other arithmetic  102 us
    dot_general x2, matrix products, per_device(): jnp.einsum('tpk,tpc->tck', code_onehot, grad_tiles, precision=lax.Precisi...  92.5 us
    all_gather x2, waiting for transfers between devices, per_device(): error_spread = lax.all_gather(error_piece, 'row', axis=1, tiled=True)  78.5 us
    all_to_all x2, blocking collectives, per_device(): lax.all_to_all(error, 'col', split_axis=1, concat_axis=0, tiled=True)  39.3 us
  transfers between devices with their start and end apart: 6, of which 5 were waited for; matrix products, arithmetic and copies ran while one was open for 12% of the time, Pallas kernels for 0%

commit v1 on v0

--- a/solution.py
+++ b/solution.py
@@ -46,7 +46,7 @@
         )
         error = rebuilt - weights.astype(jnp.float32)
         error_piece = lax.all_to_all(error, "col", split_axis=1, concat_axis=0, tiled=True)
-        error_spread = lax.all_gather(error_piece, "row", axis=1, tiled=True)
+        error_spread = jnp.concatenate(lax.all_gather(error_piece, "row"), axis=1)
         weight_grad = 2.0 * lax.psum_scatter(
             lax.dot_general(
                 error_spread,

time: 1100 us -> 1220 us (1.11)
  matrix products: 354 us -> 459 us
    dot_general x2, matrix products: 119 us -> 223 us  [per_device(): lax.dot_general(error_spread, hessian_tile, (((1,), (1,)), ((), ())), pre...]
  transfers between devices with their start and end apart: 6 -> 6, of which waited for: 5 -> 5; matrix products, arithmetic and copies ran while one was open for 12% -> 11% of each run, Pallas kernels for 0% -> 0%
where the time goes in v1:
time: 1220 us
  waiting for transfers between devices  482 us (40%)
  matrix products  459 us (38%)
  local copies, waits for them, and re-layouts  111 us (9%)
  other arithmetic  111 us (9%)
  blocking collectives  39.3 us (3%)
  between operations  13.9 us (1%)
    psum x2, waiting for transfers between devices, per_device(): lax.psum((local_grad[:, 0, :], local_grad[:, 1, :]), ('row', 'col'))  263 us
    dot_general x2, matrix products, per_device(): lax.dot_general(error_spread, hessian_tile, (((1,), (1,)), ((), ())), pre...  223 us
    reduce_scatter x2, waiting for transfers between devices, per_device(): lax.psum_scatter(lax.dot_general(error_spread, hessian_tile, (((1,), (1,)...  141 us
    dot_general x2, matrix products, per_device(): jnp.einsum('tpk,tck->tpc', code_onehot, tile_books, precision=lax.Precisi...  138 us
    unnamed x1, other arithmetic  102 us
    dot_general x2, matrix products, per_device(): jnp.einsum('tpk,tpc->tck', code_onehot, grad_tiles, precision=lax.Precisi...  92.5 us
    all_gather x2, waiting for transfers between devices, per_device(): error_spread = jnp.concatenate(lax.all_gather(error_piece, 'row'), axis=1)  78.5 us
    all_to_all x2, blocking collectives, per_device(): lax.all_to_all(error, 'col', split_axis=1, concat_axis=0, tiled=True)  39.3 us
  transfers between devices with their start and end apart: 6, of which 5 were waited for; matrix products, arithmetic and copies ran while one was open for 11% of the time, Pallas kernels for 0%

profile of v1, /device:TPU:0, one launch (start us, length us, event | category | flops | bytes accessed | tf_op | source)
XLA Modules:
  0.0 1217.0 jit_solution(11886295043134093151)
XLA Ops:
  10.8 68.2 %fusion.3 = f32[64,2048,2]{1,2,0:T(2,128)S(1)} fusion(s32[64,2048]{1,0:T(8,128)S(1)} %bitcast.78, f32[64,2,256]{2,0,1:T(8,128)S(1)} %fusion.10), kind=kOutput, calls=%fused_computation.4 | convolution fusion | flops 838860800 | bytes 1703936 | tf_op jit(solution)/shard_map/tpk,tck->tpc/dot_general | solution.py:39
  80.3 5.8 copy.27
  86.1 6.5 reshape.54
  96.3 20.4 %all_to_all.32 = f32[64,8,512]{2,0,1:T(8,128)} all-to-all(f32[64,8,512]{2,0,1:T(8,128)S(1)} %copy.29), channel_id=1, replica_groups=mesh['row'=4,'col'=8] {'col'}, dimensions={1} | all-to-all | bytes 2097152 | tf_op jit(solution)/shard_map/all_to_all | solution.py:48
  116.8 101.8 %reduce = f32[4096,4,512]{2,1,0:T(4,128)} reduce(f32[4096,4,1,512]{3,2,1,0:T(1,128)} %param.5, f32[]{:T(128)} %constant.6), dimensions={2}, to_apply=%param.5.reduce_sub_computation | reduce | bytes 67108864 | tf_op args[0]
  218.6 29.9 %copy.51 = f32[512,8,4,512]{3,1,2,0:T(8,128)} copy(f32[512,8,4,512]{3,2,1,0:T(4,128)} %bitcast.62) | data formatting | bytes 67108864
  248.6 5.2 copy.30
  253.8 111.6 %fusion.33 = f32[512,4096]{1,0:T(8,128)} fusion(f32[512,2048]{0,1:T(8,128)} %bitcast.72, f32[4096,2048]{1,0:T(8,128)} %bitcast.67), kind=kOutput, calls=%fused_computation.37 | convolution fusion | flops 51539607552 | bytes 46137344 | tf_op jit(solution)/shard_map/dot_general | solution.py:51
  365.5 71.0 %reduce-scatter.3.cloned.1.call-done = f32[64,4096]{1,0:T(8,128)} async-done(((f32[512,4096]{1,0:T(8,128)}), f32[64,4096]{1,0:T(8,128)}) %reduce-scatter.3.cloned.1.call-update) | async-done | bytes 1048592 | tf_op jit(solution)/shard_map/reduce_scatter | solution.py:50
  440.6 5.5 reshape.58
  446.1 6.7 copy.45
  453.3 46.3 %fusion.2 = f32[64,2,256]{2,1,0:T(2,128)S(1)} fusion(f32[64,2048,2]{1,2,0:T(2,128)S(1)} %reshape.71, s32[64,2048]{1,0:T(8,128)} %bitcast.79), kind=kOutput, calls=%fused_computation.3 | convolution fusion | flops 838860800 | bytes 1703936 | tf_op jit(solution)/shard_map/tpk,tpc->tck/dot_general | solution.py:67
  501.4 131.3 %all-reduce.7.cloned.1.call-done = (f32[512,1,256]{2,0,1:T(8,128)}, f32[512,1,256]{2,0,1:T(8,128)}) async-done(((f32[512,1,256]{2,0,1:T(8,128)}, f32[512,1,256]{2,0,1:T(8,128)}), (f32[512,1,256]{2,0,1:T(8,128)}, f32[512,1,256]{2,0,1:T(8,128)})) %all-reduce.7.cloned.1.call-update) | async-done | bytes 1048592 | tf_op jit(solution)/shard_map/psum | solution.py:73
  634.5 69.8 %fusion.1 = f32[64,2048,2]{1,2,0:T(2,128)} fusion(s32[64,2048]{1,0:T(8,128)} %bitcast.80, f32[64,2,256]{2,0,1:T(8,128)S(1)} %fusion.12), kind=kOutput, calls=%fused_computation.2 | convolution fusion | flops 838860800 | bytes 1703936 | tf_op jit(solution)/shard_map/tpk,tck->tpc/dot_general | solution.py:39
  706.3 5.8 copy.37
  712.1 7.6 reshape.61
  725.0 18.8 %all_to_all.33 = f32[64,8,512]{2,0,1:T(8,128)} all-to-all(f32[64,8,512]{2,0,1:T(8,128)S(1)} %copy.38), channel_id=1, replica_groups=mesh['row'=4,'col'=8] {'col'}, dimensions={1} | all-to-all | bytes 2097152 | tf_op jit(solution)/shard_map/all_to_all | solution.py:48
  743.9 78.5 %all-gather.5.cloned.1.call-done = f32[4,512,512]{2,1,0:T(8,128)} async-done(((f32[1,512,512]{2,1,0:T(8,128)}), f32[4,512,512]{2,1,0:T(8,128)}) %all-gather.5.cloned.1.call-update) | async-done | bytes 4194320 | tf_op jit(solution)/shard_map/all_gather | solution.py:49
  827.6 111.8 %fusion.34 = f32[512,4096]{1,0:T(8,128)} fusion(f32[512,2048]{0,1:T(8,128)} %bitcast.71, f32[4096,2048]{1,0:T(8,128)} %bitcast.68), kind=kOutput, calls=%fused_computation.38 | convolution fusion | flops 51539607552 | bytes 46137344 | tf_op jit(solution)/shard_map/dot_general | solution.py:51
  939.5 70.1 %reduce-scatter.5.cloned.1.call-done = f32[64,4096]{1,0:T(8,128)} async-done(((f32[512,4096]{1,0:T(8,128)}), f32[64,4096]{1,0:T(8,128)}) %reduce-scatter.5.cloned.1.call-update) | async-done | bytes 1048592 | tf_op jit(solution)/shard_map/reduce_scatter | solution.py:50
  1012.9 7.3 reshape.64
  1020.2 6.7 copy.46
  1027.4 46.3 %fusion = f32[64,2,256]{2,1,0:T(2,128)S(1)} fusion(f32[64,2048,2]{1,2,0:T(2,128)S(1)} %reshape.72, s32[64,2048]{1,0:T(8,128)} %bitcast.81), kind=kOutput, calls=%fused_computation.1 | convolution fusion | flops 838860800 | bytes 1703936 | tf_op jit(solution)/shard_map/tpk,tpc->tck/dot_general | solution.py:67
  1075.5 131.3 %all-reduce.5.cloned.1.call-done = (f32[512,1,256]{2,0,1:T(8,128)}, f32[512,1,256]{2,0,1:T(8,128)}) async-done(((f32[512,1,256]{2,0,1:T(8,128)}, f32[512,1,256]{2,0,1:T(8,128)}), (f32[512,1,256]{2,0,1:T(8,128)}, f32[512,1,256]{2,0,1:T(8,128)})) %all-reduce.5.cloned.1.call-update) | async-done | bytes 1048592 | tf_op jit(solution)/shard_map/psum | solution.py:73
  (49 shorter events, 39.1 us)
Async XLA Ops:
  6.5 242.0 %all-gather.3.cloned.1.call-start = ((), (), s32[]{:S(2)}) async-start(), calls=%async_computation.4 | async-start | bytes 5242880 | tf_op jit(solution)/shard_map/all_gather | solution.py:49
  8.8 2.0 copy-start.4
  10.8 69.1 %copy-start.3 = (bf16[64,4096]{1,0:T(8,128)(2,1)S(1)}, bf16[64,4096]{1,0:T(8,128)(2,1)}, u32[]{:S(2)}) copy-start(bf16[64,4096]{1,0:T(8,128)(2,1)} %param.6) | copy-start | bytes 1572868
  116.8 319.7 %reduce-scatter.3.cloned.1.call-start = ((), (), s32[]{:S(2)}) async-start(), calls=%async_computation.5 | async-start | bytes 9437184 | tf_op jit(solution)/shard_map/reduce_scatter | solution.py:50
  365.4 267.2 %all-reduce.7.cloned.1.call-start = ((), (), s32[]{:S(2)}) async-start(), calls=%async_computation.9 | async-start | bytes 2097152 | tf_op jit(solution)/shard_map/psum | solution.py:73
  453.3 179.4 %copy-start = (f32[512,2,256]{2,1,0:T(2,128)S(1)}, f32[512,2,256]{2,1,0:T(2,128)}, u32[]{:S(2)}) copy-start(f32[512,2,256]{2,1,0:T(2,128)} %param.9) | copy-start | bytes 3145732
  501.3 321.1 %all-gather.5.cloned.1.call-start = ((), (), s32[]{:S(2)}) async-start(), calls=%async_computation.6 | async-start | bytes 5242880 | tf_op jit(solution)/shard_map/all_gather | solution.py:49
  743.8 265.8 %reduce-scatter.5.cloned.1.call-start = ((), (), s32[]{:S(2)}) async-start(), calls=%async_computation.7 | async-start | bytes 9437184 | tf_op jit(solution)/shard_map/reduce_scatter | solution.py:50
  939.5 267.3 %all-reduce.5.cloned.1.call-start = ((), (), s32[]{:S(2)}) async-start(), calls=%async_computation.8 | async-start | bytes 2097152 | tf_op jit(solution)/shard_map/psum | solution.py:73
  1027.4 179.4 %copy-start.1 = (f32[512,1,256]{2,0,1:T(8,128)S(1)}, f32[512,1,256]{2,0,1:T(8,128)}, u32[]{:S(2)}) copy-start(f32[512,1,256]{2,0,1:T(8,128)} %get-tuple-element.7) | copy-start | bytes 1572868
  1027.4 179.4 %copy-start.2 = (f32[512,1,256]{2,0,1:T(8,128)S(1)}, f32[512,1,256]{2,0,1:T(8,128)}, u32[]{:S(2)}) copy-start(f32[512,1,256]{2,0,1:T(8,128)} %get-tuple-element.8) | copy-start | bytes 1572868
Sparse Core Ops, SparseCore 0:
  116.9 80.0 all-gather.2
  365.6 70.8 reduce-scatter.2
  501.4 131.1 all-reduce.6
  744.0 78.3 all-gather.4
  939.6 69.9 reduce-scatter.4
  1075.6 131.1 all-reduce.4
